TPU v7x, 256 devices: a whole 4x4x8 slice. The times are simulated.
256 devices in a mesh: seq: 64 (over x, z, core), head: 4 (over y).
Axes of the slice: x: 4, y: 4, z: 8, core: 2. Of those that a mesh axis runs over, the one named last changes fastest.
Arguments:
- queries: bfloat16 [32768, 4096], P('seq', 'head'), may hold values from -6 to 6
- key_input: bfloat16 [32768, 4096], P('seq', 'head'), may hold values from -6 to 6
- value_input: bfloat16 [32768, 4096], P('seq', 'head'), may hold values from -40 to 40
- gate_input: bfloat16 [32768, 4096], P('seq', 'head'), may hold values from -8 to 8
- kv_state: float32 [32, 128, 128], P('head'), may hold values from -512 to 512
- norm_gain: float32 [4096], replicated, may hold values from 0.25 to 1.75
- out_weight: bfloat16 [4096, 4096], P('head', 'seq'), may hold values from -0.09375 to 0.09375
Outputs:
- output: bfloat16 [32768, 4096], P(('seq', 'head'))
All inputs are finite; a program needn't handle non-finite values.
Results may differ from a plain program's by a relative error of at most 0.02.
Values may be sent and summed in bfloat16 or wider, within the bound.
A program may use at most 128 MiB of HBM per device.

v0:
```python
import jax
import jax.numpy as jnp
from jax import lax
from jax.sharding import PartitionSpec as P

DH = 128
BLOCK = 512


epsilon = 1e-05


def entering(value, axis, join, neutral):
    place = lax.axis_index(axis)
    gathered = lax.all_gather(value.astype(jnp.bfloat16), axis)
    state = jnp.zeros_like(value) + jnp.asarray(neutral, value.dtype)

    def one(turn, state):
        return join(state, lax.dynamic_index_in_dim(gathered, turn, 0, False).astype(value.dtype))

    return lax.fori_loop(0, place, one, state)


def add_states(earlier, later):
    return earlier + later


def gated_norm(attn_rows, gate_rows, gain_part, total_width, square_sum):
    attn_float = attn_rows.astype(jnp.float32)
    scale = lax.rsqrt(square_sum / total_width + epsilon)
    normed = attn_float * scale[:, None] * gain_part[None, :]
    return (normed * jax.nn.sigmoid(gate_rows.astype(jnp.float32))).astype(jnp.bfloat16)


def shards(queries, key_input, value_input, gate_input, kv_state, norm_gain, out_weight):
    tok_rows = queries.shape[0]
    local_width = queries.shape[1]
    local_heads = local_width // DH
    num_blocks = tok_rows // BLOCK
    block_shape = (num_blocks, BLOCK, local_heads, DH)
    q_blocks = queries.reshape(block_shape)
    k_blocks = key_input.reshape(block_shape)
    v_blocks = value_input.reshape(block_shape)
    block_states = jnp.einsum(
        "nthd,nthe->nhde", k_blocks, v_blocks, preferred_element_type=jnp.float32
    )
    own_total = jnp.sum(block_states, axis=0)
    prefix = entering(own_total, "seq", add_states, jnp.zeros_like(own_total))
    start_state = kv_state + prefix
    running = jnp.cumsum(block_states, axis=0) - block_states
    before = start_state[None] + running
    carried_part = jnp.einsum(
        "nthd,nhde->nthe", q_blocks.astype(jnp.float32), before, precision=lax.Precision.HIGHEST
    )
    scores = jnp.einsum("nthd,nshd->nhts", q_blocks, k_blocks, preferred_element_type=jnp.float32)
    causal = jnp.arange(BLOCK)[:, None] >= jnp.arange(BLOCK)[None, :]
    weights = jnp.where(causal[None, None], scores, 0.0).astype(jnp.bfloat16)
    inner_part = jnp.einsum(
        "nhts,nshe->nthe", weights, v_blocks, preferred_element_type=jnp.float32
    )
    attn = (carried_part + inner_part).astype(jnp.bfloat16).reshape(tok_rows, local_width)
    total_width = local_width * lax.axis_size("head")
    tok_attn, tok_gate = (
        lax.all_to_all(attn, "head", split_axis=0, concat_axis=1, tiled=True),
        lax.all_to_all(gate_input, "head", split_axis=0, concat_axis=1, tiled=True),
    )
    tok_float = tok_attn.astype(jnp.float32)
    normed = gated_norm(
        tok_attn, tok_gate, norm_gain, total_width, jnp.sum(tok_float * tok_float, axis=1)
    )
    hidden = lax.all_to_all(normed, "head", split_axis=1, concat_axis=0, tiled=True)
    terms = jnp.dot(
        hidden,
        lax.all_gather(out_weight, "seq", axis=1, tiled=True),
        preferred_element_type=jnp.float32,
    )
    return lax.psum_scatter(terms.astype(jnp.bfloat16), "head", scatter_dimension=0, tiled=True)


def solution(mesh):
    in_specs = (
        P("seq", "head"),
        P("seq", "head"),
        P("seq", "head"),
        P("seq", "head"),
        P("head", None, None),
        P(),
        P("head", "seq"),
    )
    out_specs = P(("seq", "head"), None)
    return jax.shard_map(shards, mesh=mesh, in_specs=in_specs, out_specs=out_specs, check_vma=False)
```

profile of v0, /device:TPU:1, one launch (start us, length us, event | category | flops | bytes accessed | tf_op | source)
XLA Modules:
  0.0 307.6 jit_solution(3969963221888918470)
XLA Ops:
  6.5 0.0 copy-start
  6.5 0.0 all-gather.6.cloned.1.call-start
  6.5 2.9 fusion.34
  9.4 0.0 all-gather.6.cloned.1.call-update
  9.4 0.0 all-gather.4.cloned.1.call-start
  9.5 0.7 all-gather.4.cloned.1.call-update
  10.2 0.1 iota_compare_fusion
  10.3 103.8 %all-gather.6.cloned.1.call-done = bf16[512,128,128]{2,1,0:T(8,128)(2,1)} async-done(((bf16[8,128,128]{2,1,0:T(8,128)(2,1)}), bf16[512,128,128]{2,1,0:T(8,128)(2,1)}) %all-gather.6.cloned.1.call-update) | async-done | bytes 16777232 | tf_op jit(solution)/shard_map/all_gather | solution.py:15
  114.1 0.0 copy-start.2
  114.1 1.2 while.10
  114.1 1.1 convert_add_fusion.2
  115.3 0.0 copy-done
  115.3 0.0 copy-done.2
  115.3 2.4 fusion.13
  117.7 4.8 %fusion.10 = bf16[1,512,8,128]{1,3,2,0:T(8,128)(2,1)S(1)} fusion(f32[8,128,512]{2,1,0:T(8,128)} %fusion.13, pred[512,512]{1,0:T(8,128)(4,1)S(1)} %iota_compare_fusion, bf16[512,1024]{1,0:T(8,128)(2,1)S(1)} %copy-done, bf16[512,1024]{1,0:T(8,128)(2,1)} %param.11, bf16[512,1024]{1,0:T(8,128)(2,1)} %param.10), kind=kOutput, calls=%fused_computation.15 | convolution fusion | flops 1078984704 | bytes 6553600 | tf_op jit(solution)/shard_map/nhts,nshe->nthe/dot_general | solution.py:58
  122.5 0.3 all_to_all.32
  122.8 0.0 copy-start.1
  122.8 1.1 copy.40
  123.9 4.0 %all-to-all-start = ((bf16[4,128,1024]{1,2,0:T(8,128)(2,1)}), bf16[4,128,1024]{1,2,0:T(8,128)(2,1)S(1)}, u32[]{:S(2)}, u32[]{:S(2)}) async-start(bf16[4,128,1024]{1,2,0:T(8,128)(2,1)} %copy.40), calls=%async_computation | async-start | bytes 2097152 | tf_op jit(solution)/shard_map/all_to_all | solution.py:64
  127.9 0.0 copy-done.1
  127.9 0.0 copy-start.3
  128.0 1.3 copy.41
  129.3 13.6 %all-to-all-done = bf16[4,128,1024]{1,2,0:T(8,128)(2,1)S(1)} async-done(((bf16[4,128,1024]{1,2,0:T(8,128)(2,1)}), bf16[4,128,1024]{1,2,0:T(8,128)(2,1)S(1)}, u32[]{:S(2)}, u32[]{:S(2)}) %all-to-all-start) | async-done | bytes 1048608 | tf_op jit(solution)/shard_map/all_to_all | solution.py:64
  142.8 3.5 %all-to-all-start.1 = ((bf16[4,128,1024]{1,2,0:T(8,128)(2,1)}), bf16[4,128,1024]{1,2,0:T(8,128)(2,1)S(1)}, u32[]{:S(2)}, u32[]{:S(2)}) async-start(bf16[4,128,1024]{1,2,0:T(8,128)(2,1)} %copy.41), calls=%async_computation.1 | async-start | bytes 2097152 | tf_op jit(solution)/shard_map/all_to_all | solution.py:65
  146.3 0.0 reduce-scatter.2.cloned.1.call-start
  146.4 0.0 copy-done.3
  146.4 0.6 fusion.5
  147.0 13.3 %all-to-all-done.1 = bf16[4,128,1024]{1,2,0:T(8,128)(2,1)S(1)} async-done(((bf16[4,128,1024]{1,2,0:T(8,128)(2,1)}), bf16[4,128,1024]{1,2,0:T(8,128)(2,1)S(1)}, u32[]{:S(2)}, u32[]{:S(2)}) %all-to-all-start.1) | async-done | bytes 1048608 | tf_op jit(solution)/shard_map/all_to_all | solution.py:65
  160.2 0.8 fusion.21
  161.0 15.2 %all_to_all.42 = bf16[128,4,1024]{0,2,1:T(8,128)(2,1)S(1)} all-to-all(bf16[128,4,1024]{0,2,1:T(8,128)(2,1)S(1)} %fusion.21), channel_id=1, replica_groups=mesh['seq'=64,'head'=4] {'head'}, dimensions={1} | all-to-all | bytes 2097152 | tf_op jit(solution)/shard_map/all_to_all | solution.py:71
  176.2 0.5 copy.42
  176.7 20.2 %all-gather.4.cloned.1.call-done = bf16[1024,4096]{0,1:T(8,128)(2,1)} async-done(((bf16[1024,64]{0,1:T(8,128)(2,1)}), bf16[1024,4096]{0,1:T(8,128)(2,1)}) %all-gather.4.cloned.1.call-update) | async-done | bytes 8388624 | tf_op jit(solution)/shard_map/all_gather | solution.py:74
  196.9 9.4 %convolution_convert_fusion = bf16[512,4096]{1,0:T(8,128)(2,1)} fusion(bf16[512,1024]{1,0:T(8,128)(2,1)S(1)} %bitcast.73, bf16[1024,4096]{0,1:T(8,128)(2,1)} %all-gather.4.cloned.1.call-done), kind=kOutput, calls=%fused_computation.2 | convolution fusion | flops 4297064448 | bytes 13631488 | tf_op jit(solution)/shard_map/dot_general | solution.py:72
  206.3 0.0 reduce-scatter.2.cloned.1.call-update
  206.4 94.8 %reduce-scatter.2.cloned.1.call-done = bf16[128,4096]{1,0:T(8,128)(2,1)} async-done(((bf16[512,4096]{1,0:T(8,128)(2,1)}), bf16[128,4096]{1,0:T(8,128)(2,1)}) %reduce-scatter.2.cloned.1.call-update) | async-done | bytes 1048592 | tf_op jit(solution)/shard_map/reduce_scatter | solution.py:77
  (3 shorter events, 0.1 us)
Async XLA Ops:
  6.5 108.7 %copy-start = (bf16[512,1024]{1,0:T(8,128)(2,1)S(1)}, bf16[512,1024]{1,0:T(8,128)(2,1)}, u32[]{:S(2)}) copy-start(bf16[512,1024]{1,0:T(8,128)(2,1)} %param.9) | copy-start | bytes 3145732
  6.5 107.5 %all-gather.6.cloned.1.call-start = ((), (), s32[]{:S(2)}) async-start(), calls=%async_computation.6 | async-start | bytes 17039360 | tf_op jit(solution)/shard_map/all_gather | solution.py:15
  9.4 187.4 %all-gather.4.cloned.1.call-start = ((), (), s32[]{:S(2)}) async-start(), calls=%async_computation.4 | async-start | bytes 8519680 | tf_op jit(solution)/shard_map/all_gather | solution.py:74
  114.1 1.2 copy-start.2
  122.8 5.1 %copy-start.1 = (bf16[512,1024]{1,0:T(8,128)(2,1)S(1)}, bf16[512,1024]{1,0:T(8,128)(2,1)}, u32[]{:S(2)}) copy-start(bf16[512,1024]{1,0:T(8,128)(2,1)} %param.12) | copy-start | bytes 3145732
  123.9 18.9 %all-to-all-start = ((bf16[4,128,1024]{1,2,0:T(8,128)(2,1)}), bf16[4,128,1024]{1,2,0:T(8,128)(2,1)S(1)}, u32[]{:S(2)}, u32[]{:S(2)}) async-start(bf16[4,128,1024]{1,2,0:T(8,128)(2,1)} %copy.40), calls=%async_computation | async-start | bytes 2097152 | tf_op jit(solution)/shard_map/all_to_all | solution.py:64
  127.9 18.4 %copy-start.3 = (f32[4096]{0:T(1024)S(1)}, f32[4096]{0:T(1024)}, u32[]{:S(2)}) copy-start(f32[4096]{0:T(1024)} %param.14) | copy-start | bytes 49156
  142.8 17.4 %all-to-all-start.1 = ((bf16[4,128,1024]{1,2,0:T(8,128)(2,1)}), bf16[4,128,1024]{1,2,0:T(8,128)(2,1)S(1)}, u32[]{:S(2)}, u32[]{:S(2)}) async-start(bf16[4,128,1024]{1,2,0:T(8,128)(2,1)} %copy.41), calls=%async_computation.1 | async-start | bytes 2097152 | tf_op jit(solution)/shard_map/all_to_all | solution.py:65
  146.3 154.8 %reduce-scatter.2.cloned.1.call-start = ((), (), s32[]{:S(2)}) async-start(), calls=%async_computation.5 | async-start | bytes 5242880 | tf_op jit(solution)/shard_map/reduce_scatter | solution.py:77
Sparse Core Ops, SparseCore 0:
  10.1 103.8 all-gather.5
  116.8 79.9 all-gather.3
  206.5 94.5 reduce-scatter.1
where the time goes:
time: 310 us; the launch traced here: 308 us
  waiting for transfers between devices  246 us (79%)
  matrix products  19.5 us (6%)
  blocking collectives  15.2 us (5%)
  between operations  13.2 us (4%)
  starting transfers between devices  7.63 us (2%)
  local copies, waits for them, and re-layouts  3.29 us (1%)
    all_gather x1, waiting for transfers between devices, entering(): gathered = lax.all_gather(value.astype(jnp.bfloat16), axis)  104 us
    reduce_scatter x1, waiting for transfers between devices, shards(): lax.psum_scatter(terms.astype(jnp.bfloat16), 'head', scatter_dimension=0,...  94.8 us
    all_gather x1, waiting for transfers between devices, shards(): lax.all_gather(out_weight, 'seq', axis=1, tiled=True)  20.2 us
    all_to_all x1, blocking collectives, shards(): lax.all_to_all(normed, 'head', split_axis=1, concat_axis=0, tiled=True)  15.2 us
    all_to_all x1, waiting for transfers between devices, shards(): lax.all_to_all(attn, 'head', split_axis=0, concat_axis=1, tiled=True)  13.6 us
    all_to_all x1, waiting for transfers between devices, shards(): lax.all_to_all(gate_input, 'head', split_axis=0, concat_axis=1, tiled=True)  13.3 us
    dot_general x1, matrix products, shards(): jnp.dot(hidden, lax.all_gather(out_weight, 'seq', axis=1, tiled=True), pr...  9.44 us
  transfers between devices with their start and end apart: 5, of which 5 were waited for; matrix products, arithmetic and copies ran while one was open for 4% of the time, Pallas kernels for 0%

commit v1 on v0

v1 whole, which is shorter than its diff:
```python
import jax
import jax.numpy as jnp
from jax import lax
from jax.experimental import pallas as pl
from jax.experimental.pallas import tpu as pltpu
from jax.sharding import PartitionSpec as P

MESH = pl.DeviceIdType.MESH
DH = 128
X, Z, Y = 4, 8, 4
EPS = 1e-05
F32, BF16 = jnp.float32, jnp.bfloat16


def dot(a, b, ca, cb):
    return lax.dot_general(a, b, (((ca,), (cb,)), ((), ())), preferred_element_type=F32)


def body(
    q_hbm, k_hbm, v_hbm, g_hbm, kv_hbm, gain_ref, w_hbm, out_ref,
    q, k, v, g, kv, w, wt,
    s_own, s_other, t_send, t_recv, line, l_send, l_recv, p_send, p_chip, c_send, c_recv,
    inner, gated, hidden, sq, sq_recv, terms,
    ra_p, ra_m, rb_p, rb_m, rc_p, rc_m,
    load, wz_s, wz_r, wx_s, wx_r, wc_s, wc_r,
    sc_s, sc_r, tz_s, tz_r, lx_s, lx_r, pz_s, pz_r, cc_s, cc_r, sq_s, sq_r,
    rs_s, rs_r,
):
    seq, y = lax.axis_index("seq"), lax.axis_index("head")
    c = lax.rem(seq, 2)
    chip = seq // 2
    z = lax.rem(chip, Z)
    x = chip // Z

    def at(xx, zz, cc):
        return {"seq": (lax.rem(xx + X, X) * Z + lax.rem(zz + Z, Z)) * 2 + cc}

    def row(step):
        return {"head": lax.rem(y + step + Y, Y)}

    partner = at(x, z, 1 - c)
    y_quarter = [pl.ds(pl.multiple_of(lax.rem(y + d, Y) * 128, 128), 128) for d in range(Y)]

    loads = [(w_hbm, w), (k_hbm, k), (v_hbm, v), (q_hbm, q), (kv_hbm, kv), (g_hbm, g)]
    copies = [pltpu.make_async_copy(a, b, load.at[i]) for i, (a, b) in enumerate(loads)]
    for copy in copies:
        copy.start()
    barrier = pltpu.get_barrier_semaphore()
    partners = [partner] + [at(x, z + d, c) for d in range(1, Z)] + [at(x + d, z, c) for d in range(1, X)]
    partners += [row(d) for d in range(1, Y)]
    for device in partners:
        pl.semaphore_signal(barrier, inc=1, device_id=device, device_id_type=MESH)
    copies[0].wait()
    eye = (
        lax.broadcasted_iota(jnp.int32, (64, 64), 0) == lax.broadcasted_iota(jnp.int32, (64, 64), 1)
    ).astype(F32).astype(BF16)
    wt[0, 0, c] = dot(eye, w[...], 1, 1).astype(BF16)
    pl.semaphore_wait(barrier, len(partners))

    def remote(src, dst, ssem, rsem, device):
        return pltpu.make_async_remote_copy(
            src_ref=src, dst_ref=dst, send_sem=ssem, recv_sem=rsem, device_id=device, device_id_type=MESH
        )

    def wz(src, dst):
        step = 1 if dst % 2 else -1
        return remote(wt.at[src, 0, c], wt.at[dst, 0, c], wz_s.at[dst], wz_r.at[dst], at(x, z + step, c))

    def wx(j, kind):
        step = 1 if kind % 2 == 0 else -1
        if kind < 2:
            src, dst = wt.at[j, 0, c], wt.at[j, 1 + kind, c]
        else:
            half = pl.ds(32 * (kind - 2), 32)
            src, dst = wt.at[j, kind - 1, c, half], wt.at[j, 3, c, half]
        return remote(src, dst, wx_s.at[j, kind], wx_r.at[j, kind], at(x + step, z, c))

    def wc(j, place):
        block = wt.at[j, place, c]
        return remote(block, block, wc_s.at[j, place], wc_r.at[j, place], partner)

    def spread(j):
        wx(j, 0).start()
        wx(j, 1).start()
        wc(j, 0).start()

    def service_z(s):
        a = 2 * s - 1
        wz(max(a - 2, 0), a).wait_recv()
        if s < 4:
            wz(a, a + 2).start()
        spread(a)
        if s < 4:
            wz(max(a - 1, 0), a + 1).wait_recv()
            if s < 3:
                wz(a + 1, a + 3).start()
            spread(a + 1)

    def service_x(j):
        wx(j, 0).wait_recv()
        wx(j, 2).start()
        wx(j, 1).wait_recv()
        wx(j, 3).start()
        wc(j, 1).start()
        wc(j, 2).start()

    def service_far(j):
        wx(j, 2).wait_recv()
        wx(j, 3).wait_recv()
        wc(j, 3).start()

    wz(0, 1).start()
    wz(0, 2).start()
    spread(0)

    copies[1].wait()
    copies[2].wait()
    for h in range(8):
        cols = slice(h * DH, (h + 1) * DH)
        s_own[h // 4, h % 4] = dot(k[:, cols], v[:, cols], 0, 0)
    state_swap = remote(s_own.at[1 - c], s_other, sc_s, sc_r, partner)
    state_swap.start()

    copies[3].wait()
    lower = lax.broadcasted_iota(jnp.int32, (256, 256), 0) >= lax.broadcasted_iota(jnp.int32, (256, 256), 1)

    def local(h):
        cols = slice(h * DH, (h + 1) * DH)
        for r in range(2):
            rows = slice(r * 256, (r + 1) * 256)
            q_rows = q[rows, cols]
            near = jnp.where(lower, dot(q_rows, k[rows, cols], 1, 1), 0.0).astype(BF16)
            total = dot(near, v[rows, cols], 1, 0)
            if r == 1:
                far = dot(q_rows, k[0:256, cols], 1, 1).astype(BF16)
                total = total + dot(far, v[0:256, cols], 1, 0)
            inner[rows, cols] = total

    local(0)
    state_swap.wait_recv()
    for h in range(4):
        t = (s_own[c, h] + s_other[h]).astype(BF16)
        t_send[2 * h] = t[0:64]
        t_send[2 * h + 1] = t[64:128]

    def tz(d):
        to = lax.rem(z + d, Z)
        return remote(t_send.at[to], t_recv.at[z], tz_s.at[d], tz_r.at[d], at(x, z + d, c))

    def pz(d):
        to = lax.rem(z + d, Z)
        return remote(p_send.at[to], p_chip.at[z], pz_s.at[d], pz_r.at[d], at(x, z + d, c))

    def lx(d):
        return remote(l_send, l_recv.at[d], lx_s.at[d], lx_r.at[d], at(x + d, z, c))

    for d in (4, 3, 5, 2, 6, 1, 7):
        tz(d).start()
    t_recv[z] = t_send[z]
    service_z(1)
    local(1)
    local(2)
    local(3)
    for d in range(1, Z):
        tz(d).wait_recv()
    total = jnp.zeros((64, DH), F32)
    for i in range(Z):
        line[i] = total
        total = total + t_recv[i].astype(F32)
    l_send[...] = total.astype(BF16)
    for d in (2, 1, 3):
        lx(d).start()
    service_z(2)
    service_x(0)
    local(4)
    for d in range(1, X):
        lx(d).wait_recv()
    before = jnp.zeros((64, DH), F32)
    for d in range(1, X):
        before = before + jnp.where(x >= d, l_recv[d].astype(F32), 0.0)
    for i in range(Z):
        p_send[i] = (line[i] + before).astype(BF16)
    for d in (4, 3, 5, 2, 6, 1, 7):
        pz(d).start()
    p_chip[z] = p_send[z]
    service_z(3)
    local(5)
    local(6)
    local(7)
    service_x(1)
    service_far(0)
    copies[5].wait()
    for i in range(4):
        rows = slice(i * 128, (i + 1) * 128)
        gated[rows] = gain_ref[...] * jax.nn.sigmoid(g[rows].astype(F32))
    service_z(4)
    copies[4].wait()
    for d in range(1, Z):
        pz(d).wait_recv()
    own_part = (1 - c).astype(F32)
    other_part = c.astype(F32)
    for h in range(4):
        base = jnp.concatenate([p_chip[2 * h].astype(F32), p_chip[2 * h + 1].astype(F32)], axis=0)
        c_send[h] = base + own_part * s_own[c, h]
        s_other[h] = base + other_part * s_other[h]
    prefix_swap = remote(c_send, c_recv, cc_s, cc_r, partner)
    prefix_swap.start()

    def carried(h, state):
        hi = state.astype(BF16)
        lo = (state - hi.astype(F32)).astype(BF16)
        return jnp.concatenate([hi, lo], axis=0)

    def finish(half, first):
        prefix = s_other if half == 0 else c_recv
        which = c if half == 0 else 1 - c
        for h in range(4):
            state = carried(h, kv[which * 4 + h] + prefix[h])
            cols = pl.ds(pl.multiple_of((which * 4 + h) * DH, DH), DH)
            qq = q[:, cols]
            attn = inner[:, cols] + dot(jnp.concatenate([qq, qq], axis=1), state, 1, 0)
            attn = attn.astype(BF16).astype(F32)
            square = attn * attn
            if first and h == 0:
                sq[...] = square
            else:
                sq[...] += square
            hidden[:, cols] = (attn * gated[:, cols]).astype(BF16)

    finish(0, True)
    service_x(2)
    service_far(1)
    prefix_swap.wait_recv()
    finish(1, False)
    sq[...] = jnp.broadcast_to(jnp.sum(sq[...], axis=1, keepdims=True), (512, 128))

    def sqs(d):
        return remote(sq.at[y_quarter[d]], sq_recv.at[d], sq_s.at[d], sq_r.at[d], row(d))

    for d in range(1, Y):
        sqs(d).start()

    def rs(j, kind):
        src, dst, step = {
            0: (terms.at[j, 0, y_quarter[2]], ra_p.at[j], 1),
            1: (terms.at[j, 1, y_quarter[2]], ra_m.at[j], 3),
            2: (terms.at[j, 1, y_quarter[1]], rc_p.at[j], 1),
            3: (terms.at[j, 0, y_quarter[3]], rc_m.at[j], 3),
            4: (terms.at[j, 0, y_quarter[1]], rb_p.at[j], 1),
            5: (terms.at[j, 1, y_quarter[3]], rb_m.at[j], 3),
        }[kind]
        return remote(src, dst, rs_s.at[j, kind], rs_r.at[j, kind], row(step))

    def project(j):
        for place in range(4):
            wc(j, place).wait_recv()
        for side in range(2):
            weights = wt[j, pl.ds(2 * side, 2)].reshape(256, 1024)
            terms[j, side] = dot(hidden[...], weights, 1, 1).astype(BF16)
        for kind in range(4):
            rs(j, kind).start()

    def relay(j):
        for side, part, kind in ((0, ra_p, 0), (1, ra_m, 1)):
            rs(j, kind).wait_recv()
            rows = y_quarter[1 if side == 0 else 3]
            terms[j, side, rows] = (terms[j, side, rows].astype(F32) + part[j].astype(F32)).astype(BF16)
            rs(j, 4 + side).start()

    def final(j, scale):
        for kind in (2, 3, 4, 5):
            rs(j, kind).wait_recv()
        s = (j + 1) // 2
        zz = lax.rem(z + s * (1 - 2 * lax.rem(j, 2)) + Z, Z)
        for side, b, d in ((0, rb_p, rc_m), (1, rb_m, rc_p)):
            total = terms[j, side, y_quarter[0]].astype(F32) + b[j].astype(F32) + d[j].astype(F32)
            for n in range(2):
                xx = lax.rem(x + (0, 3, 1, 2)[2 * side + n], X)
                cols = pl.ds(pl.multiple_of((xx * Z + zz) * 128, 128), 128)
                out_ref[:, cols] = (total[:, n * 128:(n + 1) * 128] * scale).astype(BF16)

    def step(i, _):
        @pl.when(i < 5)
        def _():
            service_x(i + 3)

        @pl.when(i < 6)
        def _():
            service_far(i + 2)

        @pl.when(i < 8)
        def _():
            project(i)

        @pl.when((i >= 1) & (i < 9))
        def _():
            relay(i - 1)

        @pl.when(i == 1)
        def _():
            for d in range(1, Y):
                sqs(d).wait()
            total = sq[y_quarter[0]] + sq_recv[1] + sq_recv[2] + sq_recv[3]
            sq_recv[0] = lax.rsqrt(total / (Y * 1024) + EPS)

        @pl.when(i >= 2)
        def _():
            final(i - 2, sq_recv[0])

        return 0

    lax.fori_loop(0, 10, step, 0)

    for dst in range(1, Z):
        wz(max(dst - 2, 0), dst).wait_send()
    state_swap.wait_send()
    prefix_swap.wait_send()
    for d in range(1, Z):
        tz(d).wait_send()
        pz(d).wait_send()
    for d in range(1, X):
        lx(d).wait_send()

    def drain(j, _):
        for kind in range(4):
            wx(j, kind).wait_send()
            wc(j, kind).wait_send()
        for kind in range(6):
            rs(j, kind).wait_send()
        return 0

    lax.fori_loop(0, 8, drain, 0)


def shards(queries, key_input, value_input, gate_input, kv_state, norm_gain, out_weight):
    y = lax.axis_index("head")
    gain = lax.dynamic_slice_in_dim(norm_gain, y * 1024, 1024).reshape(1, 1024)
    hbm = pl.BlockSpec(memory_space=pl.ANY)
    vmem = pl.BlockSpec(memory_space=pltpu.VMEM)
    dma = pltpu.SemaphoreType.DMA
    scratch = [
        pltpu.VMEM((512, 1024), BF16), pltpu.VMEM((512, 1024), BF16), pltpu.VMEM((512, 1024), BF16),
        pltpu.VMEM((512, 1024), BF16), pltpu.VMEM((8, DH, DH), F32), pltpu.VMEM((1024, 64), BF16),
        pltpu.VMEM((Z, X, 2, 64, 1024), BF16),
        pltpu.VMEM((2, 4, DH, DH), F32), pltpu.VMEM((4, DH, DH), F32),
        pltpu.VMEM((Z, 64, DH), BF16), pltpu.VMEM((Z, 64, DH), BF16), pltpu.VMEM((Z, 64, DH), F32),
        pltpu.VMEM((64, DH), BF16), pltpu.VMEM((X, 64, DH), BF16),
        pltpu.VMEM((Z, 64, DH), BF16), pltpu.VMEM((Z, 64, DH), BF16),
        pltpu.VMEM((4, DH, DH), F32), pltpu.VMEM((4, DH, DH), F32),
        pltpu.VMEM((512, 1024), F32), pltpu.VMEM((512, 1024), F32), pltpu.VMEM((512, 1024), BF16),
        pltpu.VMEM((512, 128), F32), pltpu.VMEM((Y, 128, 128), F32),
        pltpu.VMEM((Z, 2, 512, 256), BF16),
    ] + [pltpu.VMEM((Z, 128, 256), BF16)] * 6 + [
        dma((6,)), dma((Z,)), dma((Z,)), dma((Z, 4)), dma((Z, 4)), dma((Z, 4)), dma((Z, 4)),
        dma, dma, dma((Z,)), dma((Z,)), dma((X,)), dma((X,)), dma((Z,)), dma((Z,)),
        dma, dma, dma((Y,)), dma((Y,)), dma((Z, 6)), dma((Z, 6)),
    ]
    return pl.pallas_call(
        body,
        out_shape=jax.ShapeDtypeStruct((128, 4096), BF16),
        in_specs=[hbm, hbm, hbm, hbm, hbm, vmem, hbm],
        out_specs=vmem,
        scratch_shapes=scratch,
        compiler_params=pltpu.CompilerParams(
            collective_id=0, has_side_effects=True, vmem_limit_bytes=48 << 20
        ),
        name="layer",
    )(queries, key_input, value_input, gate_input, kv_state, gain, out_weight)


def solution(mesh):
    in_specs = (
        P("seq", "head"),
        P("seq", "head"),
        P("seq", "head"),
        P("seq", "head"),
        P("head", None, None),
        P(),
        P("head", "seq"),
    )
    out_specs = P(("seq", "head"), None)
    return jax.shard_map(shards, mesh=mesh, in_specs=in_specs, out_specs=out_specs, check_vma=False)
```

time: 310 us -> 88.8 us (0.29)
  waiting for transfers between devices: 246 us -> 0 us
  Pallas kernels: 0 us -> 78.4 us
  matrix products: 19.5 us -> 0 us
  blocking collectives: 15.2 us -> 0 us
  between operations: 13.2 us -> 0.03 us
  starting transfers between devices: 7.63 us -> 0 us
  local copies, waits for them, and re-layouts: 3.29 us -> 8.67 us
    all_gather x2 -> x0, waiting for transfers between devices: 124 us -> none  [the longest x1 104 us: entering(): gathered = lax.all_gather(value.astype(jnp.bfloat16), axis)]
    reduce_scatter x1 -> x0, waiting for transfers between devices: 94.8 us -> none  [shards(): lax.psum_scatter(terms.astype(jnp.bfloat16), 'head', scatter_dimension=0,...]
    pallas_call x0 -> x1, Pallas kernels: none -> 78.4 us  [shards(): pl.pallas_call(body, out_shape=jax.ShapeDtypeStruct((128, 4096), BF16), i...]
    all_to_all x2 -> x0, waiting for transfers between devices: 26.8 us -> none  [the longest x1 13.6 us: shards(): lax.all_to_all(attn, 'head', split_axis=0, concat_axis=1, tiled=True)]
    dot_general x4 -> x0, matrix products: 19.5 us -> none  [the longest x1 9.44 us: shards(): jnp.dot(hidden, lax.all_gather(out_weight, 'seq', axis=1, tiled=True), pr...]
    all_to_all x1 -> x0, blocking collectives: 15.2 us -> none  [shards(): lax.all_to_all(normed, 'head', split_axis=1, concat_axis=0, tiled=True)]
    unnamed x8 -> x12, local copies, waits for them, and re-layouts: 0.02 us -> 7.98 us
    all_to_all x2 -> x0, starting transfers between devices: 7.54 us -> none  [the longest x1 4.02 us: shards(): lax.all_to_all(attn, 'head', split_axis=0, concat_axis=1, tiled=True)]
  transfers between devices with their start and end apart: 5 -> 0, of which waited for: 5 -> 0; matrix products, arithmetic and copies ran while one was open for 4% -> 0% of each run, Pallas kernels for 0% -> 0%
where the time goes in v1:
time: 88.8 us; the launch traced here: 87.1 us
  Pallas kernels  78.4 us (88%)
  local copies, waits for them, and re-layouts  8.67 us (10%)
    pallas_call x1, Pallas kernels, shards(): pl.pallas_call(body, out_shape=jax.ShapeDtypeStruct((128, 4096), BF16), i...  78.4 us
    unnamed x12, local copies, waits for them, and re-layouts  7.98 us

profile of v1, /device:TPU:1, one launch (start us, length us, event | category | flops | bytes accessed | tf_op | source)
XLA Modules:
  0.0 87.1 jit_solution(8145199211249027463)
XLA Ops:
  0.0 0.7 dynamic_slice.3
  0.7 1.1 %copy.8.w_hbm = bf16[1024,64]{1,0:T(8,128)(2,1)S(1)} copy(bf16[1024,64]{0,1:T(8,128)(2,1)} %param.13) | data formatting | bytes 262144 | tf_op args[6]
  1.8 0.0 copy-start
  1.8 1.2 %copy-done = bf16[512,1024]{1,0:T(8,128)(2,1)S(1)} copy-done((bf16[512,1024]{1,0:T(8,128)(2,1)S(1)}, bf16[512,1024]{1,0:T(8,128)(2,1)}, u32[]{:S(2)}) %copy-start) | copy-done | bytes 1048600
  3.0 0.0 copy-start.1
  3.0 1.2 %copy-done.1 = bf16[512,1024]{1,0:T(8,128)(2,1)S(1)} copy-done((bf16[512,1024]{1,0:T(8,128)(2,1)S(1)}, bf16[512,1024]{1,0:T(8,128)(2,1)}, u32[]{:S(2)}) %copy-start.1) | copy-done | bytes 1048600
  4.2 0.0 copy-start.2
  4.2 1.2 %copy-done.2 = bf16[512,1024]{1,0:T(8,128)(2,1)S(1)} copy-done((bf16[512,1024]{1,0:T(8,128)(2,1)S(1)}, bf16[512,1024]{1,0:T(8,128)(2,1)}, u32[]{:S(2)}) %copy-start.2) | copy-done | bytes 1048600
  5.4 0.0 copy-start.3
  5.4 1.2 %copy-done.3 = bf16[512,1024]{1,0:T(8,128)(2,1)S(1)} copy-done((bf16[512,1024]{1,0:T(8,128)(2,1)S(1)}, bf16[512,1024]{1,0:T(8,128)(2,1)}, u32[]{:S(2)}) %copy-start.3) | copy-done | bytes 1048600
  6.7 0.0 copy-start.4
  6.7 1.0 %copy-done.4 = f32[8,128,128]{2,1,0:T(8,128)S(1)} copy-done((f32[8,128,128]{2,1,0:T(8,128)S(1)}, f32[8,128,128]{2,1,0:T(8,128)}, u32[]{:S(2)}) %copy-start.4) | copy-done | bytes 524312
  7.7 78.4 %layer.1 = bf16[128,4096]{1,0:T(8,128)(2,1)S(1)} custom-call(bf16[512,1024]{1,0:T(8,128)(2,1)S(1)} %copy-done, bf16[512,1024]{1,0:T(8,128)(2,1)S(1)} %copy-done.1, bf16[512,1024]{1,0:T(8,128)(2,1)S(1)} %copy-done.2, bf16[512,1024]{1,0:T(8,128)(2,1)S(1)} %copy-done.3, f32[8,128,128]{2,1,0:T(8,128)S(1)} %copy-done.4, f32[1,1024]{1,0:T(1,128)S(1)} %bitcast.1, ...), custom_call_target="tpu_custom_call" | custom-call | tf_op jit(solution)/shard_map/layer/pallas_call | solution.py:358
  86.2 1.0 %copy.10 = bf16[128,4096]{1,0:T(8,128)(2,1)} copy(bf16[128,4096]{1,0:T(8,128)(2,1)S(1)} %layer.1) | data formatting | bytes 2097152
Async XLA Ops:
  1.8 1.2 %copy-start = (bf16[512,1024]{1,0:T(8,128)(2,1)S(1)}, bf16[512,1024]{1,0:T(8,128)(2,1)}, u32[]{:S(2)}) copy-start(bf16[512,1024]{1,0:T(8,128)(2,1)} %q_hbm.1) | copy-start | bytes 3145732
  3.0 1.2 %copy-start.1 = (bf16[512,1024]{1,0:T(8,128)(2,1)S(1)}, bf16[512,1024]{1,0:T(8,128)(2,1)}, u32[]{:S(2)}) copy-start(bf16[512,1024]{1,0:T(8,128)(2,1)} %k_hbm.1) | copy-start | bytes 3145732
  4.2 1.2 %copy-start.2 = (bf16[512,1024]{1,0:T(8,128)(2,1)S(1)}, bf16[512,1024]{1,0:T(8,128)(2,1)}, u32[]{:S(2)}) copy-start(bf16[512,1024]{1,0:T(8,128)(2,1)} %v_hbm.1) | copy-start | bytes 3145732
  5.4 1.2 %copy-start.3 = (bf16[512,1024]{1,0:T(8,128)(2,1)S(1)}, bf16[512,1024]{1,0:T(8,128)(2,1)}, u32[]{:S(2)}) copy-start(bf16[512,1024]{1,0:T(8,128)(2,1)} %g_hbm.1) | copy-start | bytes 3145732
  6.7 1.0 %copy-start.4 = (f32[8,128,128]{2,1,0:T(8,128)S(1)}, f32[8,128,128]{2,1,0:T(8,128)}, u32[]{:S(2)}) copy-start(f32[8,128,128]{2,1,0:T(8,128)} %kv_hbm.1) | copy-start | bytes 1572868

commit v2 on v1

--- a/solution.py
+++ b/solution.py
@@ -8,6 +8,7 @@
 MESH = pl.DeviceIdType.MESH
 DH = 128
 X, Z, Y = 4, 8, 4
+SPLIT = 384
 EPS = 1e-05
 F32, BF16 = jnp.float32, jnp.bfloat16
 
@@ -17,8 +18,8 @@
 
 
 def body(
-    q_hbm, k_hbm, v_hbm, g_hbm, kv_hbm, gain_ref, w_hbm, out_ref,
-    q, k, v, g, kv, w, wt,
+    q_hbm, k_hbm, v_hbm, g_hbm, kv_hbm, gain_hbm, w_hbm, out_ref,
+    q, k, v, g, kv, gain, wt,
     s_own, s_other, t_send, t_recv, line, l_send, l_recv, p_send, p_chip, c_send, c_recv,
     inner, gated, hidden, sq, sq_recv, terms,
     ra_p, ra_m, rb_p, rb_m, rc_p, rc_m,
@@ -41,7 +42,8 @@
     partner = at(x, z, 1 - c)
     y_quarter = [pl.ds(pl.multiple_of(lax.rem(y + d, Y) * 128, 128), 128) for d in range(Y)]
 
-    loads = [(w_hbm, w), (k_hbm, k), (v_hbm, v), (q_hbm, q), (kv_hbm, kv), (g_hbm, g)]
+    own_gain = gain_hbm.at[:, pl.ds(pl.multiple_of(y * 1024, 1024), 1024)]
+    loads = [(w_hbm, wt.at[0, 0, c]), (k_hbm, k), (v_hbm, v), (q_hbm, q), (kv_hbm, kv), (g_hbm, g), (own_gain, gain)]
     copies = [pltpu.make_async_copy(a, b, load.at[i]) for i, (a, b) in enumerate(loads)]
     for copy in copies:
         copy.start()
@@ -50,76 +52,102 @@
     partners += [row(d) for d in range(1, Y)]
     for device in partners:
         pl.semaphore_signal(barrier, inc=1, device_id=device, device_id_type=MESH)
-    copies[0].wait()
-    eye = (
-        lax.broadcasted_iota(jnp.int32, (64, 64), 0) == lax.broadcasted_iota(jnp.int32, (64, 64), 1)
-    ).astype(F32).astype(BF16)
-    wt[0, 0, c] = dot(eye, w[...], 1, 1).astype(BF16)
-    pl.semaphore_wait(barrier, len(partners))
-
     def remote(src, dst, ssem, rsem, device):
         return pltpu.make_async_remote_copy(
             src_ref=src, dst_ref=dst, send_sem=ssem, recv_sem=rsem, device_id=device, device_id_type=MESH
         )
 
-    def wz(src, dst):
-        step = 1 if dst % 2 else -1
-        return remote(wt.at[src, 0, c], wt.at[dst, 0, c], wz_s.at[dst], wz_r.at[dst], at(x, z + step, c))
-
-    def wx(j, kind):
-        step = 1 if kind % 2 == 0 else -1
-        if kind < 2:
-            src, dst = wt.at[j, 0, c], wt.at[j, 1 + kind, c]
-        else:
-            half = pl.ds(32 * (kind - 2), 32)
-            src, dst = wt.at[j, kind - 1, c, half], wt.at[j, 3, c, half]
-        return remote(src, dst, wx_s.at[j, kind], wx_r.at[j, kind], at(x + step, z, c))
-
-    def wc(j, place):
-        block = wt.at[j, place, c]
-        return remote(block, block, wc_s.at[j, place], wc_r.at[j, place], partner)
+    part = (slice(0, SPLIT), slice(SPLIT, 1024))
+
+    def wz(place, dst, which):
+        src = dst - 2 if dst > 2 else 0
+        index = place if which == 0 else 4
+        return remote(
+            wt.at[src, place, c, :, part[which]], wt.at[dst, place, c, :, part[which]],
+            wz_s.at[index, dst], wz_r.at[index, dst], at(x, z + (1 if dst % 2 else -1), c),
+        )
+
+    def wx(j, kind, which):
+        rows = pl.ds(0, 64) if kind < 2 else pl.ds(32 * (kind - 2), 32)
+        src, dst = (0, 1 + kind) if kind < 2 else (kind - 1, 3)
+        index = 8 if which == 0 else j
+        return remote(
+            wt.at[j, src, c, rows, part[which]], wt.at[j, dst, c, rows, part[which]],
+            wx_s.at[index, kind], wx_r.at[index, kind], at(x + (1 if kind % 2 == 0 else -1), z, c),
+        )
+
+    def wc(j):
+        block = wt.at[j, :, c]
+        return remote(block, block, wc_s.at[j], wc_r.at[j], partner)
 
     def spread(j):
-        wx(j, 0).start()
-        wx(j, 1).start()
-        wc(j, 0).start()
-
-    def service_z(s):
-        a = 2 * s - 1
-        wz(max(a - 2, 0), a).wait_recv()
-        if s < 4:
-            wz(a, a + 2).start()
-        spread(a)
-        if s < 4:
-            wz(max(a - 1, 0), a + 1).wait_recv()
-            if s < 3:
-                wz(a + 1, a + 3).start()
-            spread(a + 1)
-
-    def service_x(j):
-        wx(j, 0).wait_recv()
-        wx(j, 2).start()
-        wx(j, 1).wait_recv()
-        wx(j, 3).start()
-        wc(j, 1).start()
-        wc(j, 2).start()
-
-    def service_far(j):
-        wx(j, 2).wait_recv()
-        wx(j, 3).wait_recv()
-        wc(j, 3).start()
-
-    wz(0, 1).start()
-    wz(0, 2).start()
-    spread(0)
+        wx(j, 0, 1).start()
+        wx(j, 1, 1).start()
+
+    def start_weights():
+        for dst in (1, 2):
+            wz(0, dst, 1).start()
+        for kind in (0, 1):
+            wx(0, kind, 0).start()
+        spread(0)
+        for dst in (1, 2):
+            wz(0, dst, 0).start()
+
+    def ring_z(s, place, which):
+        for dst in (2 * s - 1, 2 * s):
+            if dst < 8:
+                wz(place, dst, which).wait_recv()
+                if dst < 6:
+                    wz(place, dst + 2, which).start()
+
+    def service_b(s):
+        ring_z(s, 0, 1)
+        for j in (2 * s - 1, 2 * s):
+            if j < 8:
+                spread(j)
+
+    def service_a(s):
+        for place in range(4):
+            ring_z(s, place, 0)
+
+    def near_a():
+        for kind in (0, 1):
+            wx(0, kind, 0).wait_recv()
+            wx(0, kind + 2, 0).start()
+        for dst in (1, 2):
+            for place in (1, 2):
+                wz(place, dst, 0).start()
+
+    def far_a():
+        for kind in (2, 3):
+            wx(0, kind, 0).wait_recv()
+        for dst in (1, 2):
+            wz(3, dst, 0).start()
+
+    def near(j):
+        for kind in (0, 1):
+            wx(j, kind, 1).wait_recv()
+            wx(j, kind + 2, 1).start()
+
+    def far(j):
+        for kind in (2, 3):
+            wx(j, kind, 1).wait_recv()
+        wc(j).start()
+
+    def states(which):
+        for h in range(4):
+            cols = pl.ds(pl.multiple_of((which * 4 + h) * DH, DH), DH)
+            s_own[which, h] = dot(k[:, cols], v[:, cols], 0, 0)
 
     copies[1].wait()
     copies[2].wait()
-    for h in range(8):
-        cols = slice(h * DH, (h + 1) * DH)
-        s_own[h // 4, h % 4] = dot(k[:, cols], v[:, cols], 0, 0)
+    states(1 - c)
+    pl.semaphore_wait(barrier, len(partners))
     state_swap = remote(s_own.at[1 - c], s_other, sc_s, sc_r, partner)
     state_swap.start()
+    copies[0].wait()
+    start_weights()
+    states(c)
 
     copies[3].wait()
     lower = lax.broadcasted_iota(jnp.int32, (256, 256), 0) >= lax.broadcasted_iota(jnp.int32, (256, 256), 1)
@@ -157,9 +185,9 @@
     for d in (4, 3, 5, 2, 6, 1, 7):
         tz(d).start()
     t_recv[z] = t_send[z]
-    service_z(1)
     local(1)
     local(2)
+    service_b(1)
     local(3)
     for d in range(1, Z):
         tz(d).wait_recv()
@@ -170,8 +198,9 @@
     l_send[...] = total.astype(BF16)
     for d in (2, 1, 3):
         lx(d).start()
-    service_z(2)
-    service_x(0)
+    near_a()
+    service_b(2)
+    near(0)
     local(4)
     for d in range(1, X):
         lx(d).wait_recv()
@@ -183,17 +212,19 @@
     for d in (4, 3, 5, 2, 6, 1, 7):
         pz(d).start()
     p_chip[z] = p_send[z]
-    service_z(3)
+    far_a()
+    far(0)
+    service_b(3)
     local(5)
     local(6)
     local(7)
-    service_x(1)
-    service_far(0)
+    near(1)
     copies[5].wait()
+    copies[6].wait()
     for i in range(4):
         rows = slice(i * 128, (i + 1) * 128)
-        gated[rows] = gain_ref[...] * jax.nn.sigmoid(g[rows].astype(F32))
-    service_z(4)
+        gated[rows] = gain[...] * jax.nn.sigmoid(g[rows].astype(F32))
+    near(2)
     copies[4].wait()
     for d in range(1, Z):
         pz(d).wait_recv()
@@ -228,8 +259,9 @@
             hidden[:, cols] = (attn * gated[:, cols]).astype(BF16)
 
     finish(0, True)
-    service_x(2)
-    service_far(1)
+    service_b(4)
+    service_a(1)
+    far(1)
     prefix_swap.wait_recv()
     finish(1, False)
     sq[...] = jnp.broadcast_to(jnp.sum(sq[...], axis=1, keepdims=True), (512, 128))
@@ -252,8 +284,7 @@
         return remote(src, dst, rs_s.at[j, kind], rs_r.at[j, kind], row(step))
 
     def project(j):
-        for place in range(4):
-            wc(j, place).wait_recv()
+        wc(j).wait_recv()
         for side in range(2):
             weights = wt[j, pl.ds(2 * side, 2)].reshape(256, 1024)
             terms[j, side] = dot(hidden[...], weights, 1, 1).astype(BF16)
@@ -280,13 +311,37 @@
                 out_ref[:, cols] = (total[:, n * 128:(n + 1) * 128] * scale).astype(BF16)
 
     def step(i, _):
-        @pl.when(i < 5)
-        def _():
-            service_x(i + 3)
-
-        @pl.when(i < 6)
-        def _():
-            service_far(i + 2)
+        @pl.when(i == 0)
+        def _():
+            near(3)
+            far(2)
+
+        @pl.when(i == 1)
+        def _():
+            near(4)
+            service_a(2)
+            far(3)
+
+        @pl.when(i == 2)
+        def _():
+            near(5)
+            far(4)
+
+        @pl.when(i == 3)
+        def _():
+            near(6)
+            service_a(3)
+            far(5)
+
+        @pl.when(i == 4)
+        def _():
+            near(7)
+            far(6)
+
+        @pl.when(i == 5)
+        def _():
+            service_a(4)
+            far(7)
 
         @pl.when(i < 8)
         def _():
@@ -312,7 +367,11 @@
     lax.fori_loop(0, 10, step, 0)
 
     for dst in range(1, Z):
-        wz(max(dst - 2, 0), dst).wait_send()
+        wz(0, dst, 1).wait_send()
+        for place in range(4):
+            wz(place, dst, 0).wait_send()
+    for kind in range(4):
+        wx(0, kind, 0).wait_send()
     state_swap.wait_send()
     prefix_swap.wait_send()
     for d in range(1, Z):
@@ -323,8 +382,8 @@
 
     def drain(j, _):
         for kind in range(4):
-            wx(j, kind).wait_send()
-            wc(j, kind).wait_send()
+            wx(j, kind, 1).wait_send()
+        wc(j).wait_send()
         for kind in range(6):
             rs(j, kind).wait_send()
         return 0
@@ -333,14 +392,12 @@
 
 
 def shards(queries, key_input, value_input, gate_input, kv_state, norm_gain, out_weight):
-    y = lax.axis_index("head")
-    gain = lax.dynamic_slice_in_dim(norm_gain, y * 1024, 1024).reshape(1, 1024)
-    hbm = pl.BlockSpec(memory_space=pl.ANY)
+    hbm = pl.BlockSpec(memory_space=pltpu.HBM)
     vmem = pl.BlockSpec(memory_space=pltpu.VMEM)
     dma = pltpu.SemaphoreType.DMA
     scratch = [
         pltpu.VMEM((512, 1024), BF16), pltpu.VMEM((512, 1024), BF16), pltpu.VMEM((512, 1024), BF16),
-        pltpu.VMEM((512, 1024), BF16), pltpu.VMEM((8, DH, DH), F32), pltpu.VMEM((1024, 64), BF16),
+        pltpu.VMEM((512, 1024), BF16), pltpu.VMEM((8, DH, DH), F32), pltpu.VMEM((1, 1024), F32),
         pltpu.VMEM((Z, X, 2, 64, 1024), BF16),
         pltpu.VMEM((2, 4, DH, DH), F32), pltpu.VMEM((4, DH, DH), F32),
         pltpu.VMEM((Z, 64, DH), BF16), pltpu.VMEM((Z, 64, DH), BF16), pltpu.VMEM((Z, 64, DH), F32),
@@ -351,21 +408,21 @@
         pltpu.VMEM((512, 128), F32), pltpu.VMEM((Y, 128, 128), F32),
         pltpu.VMEM((Z, 2, 512, 256), BF16),
     ] + [pltpu.VMEM((Z, 128, 256), BF16)] * 6 + [
-        dma((6,)), dma((Z,)), dma((Z,)), dma((Z, 4)), dma((Z, 4)), dma((Z, 4)), dma((Z, 4)),
+        dma((7,)), dma((5, Z)), dma((5, Z)), dma((Z + 1, 4)), dma((Z + 1, 4)), dma((Z,)), dma((Z,)),
         dma, dma, dma((Z,)), dma((Z,)), dma((X,)), dma((X,)), dma((Z,)), dma((Z,)),
         dma, dma, dma((Y,)), dma((Y,)), dma((Z, 6)), dma((Z, 6)),
     ]
     return pl.pallas_call(
         body,
         out_shape=jax.ShapeDtypeStruct((128, 4096), BF16),
-        in_specs=[hbm, hbm, hbm, hbm, hbm, vmem, hbm],
+        in_specs=[hbm] * 7,
         out_specs=vmem,
         scratch_shapes=scratch,
         compiler_params=pltpu.CompilerParams(
-            collective_id=0, has_side_effects=True, vmem_limit_bytes=48 << 20
+            collective_id=0, has_side_effects=True, vmem_limit_bytes=60 << 20
         ),
         name="layer",
-    )(queries, key_input, value_input, gate_input, kv_state, gain, out_weight)
+    )(queries, key_input, value_input, gate_input, kv_state, norm_gain.reshape(1, 4096), out_weight.T)
 
 
 def solution(mesh):

time: 88.8 us -> 75.9 us (0.85)
  local copies, waits for them, and re-layouts: 8.67 us -> 2.29 us
  Pallas kernels: 78.4 us -> 72.2 us
    pallas_call x1, Pallas kernels: 78.4 us -> 72.2 us  [shards(): pl.pallas_call(body, out_shape=jax.ShapeDtypeStruct((128, 4096), BF16), i...]
    unnamed x12 -> x1, local copies, waits for them, and re-layouts: 7.98 us -> 2.29 us
where the time goes in v2:
time: 75.9 us; the launch traced here: 74.5 us
  Pallas kernels  72.2 us (95%)
  local copies, waits for them, and re-layouts  2.29 us (3%)
    pallas_call x1, Pallas kernels, shards(): pl.pallas_call(body, out_shape=jax.ShapeDtypeStruct((128, 4096), BF16), i...  72.2 us
    unnamed x1, local copies, waits for them, and re-layouts  2.29 us

profile of v2, /device:TPU:1, one launch (start us, length us, event | category | flops | bytes accessed | tf_op | source)
XLA Modules:
  0.0 74.5 jit_solution(6281550315966436010)
XLA Ops:
  0.0 72.2 %layer.1 = bf16[128,4096]{1,0:T(8,128)(2,1)} custom-call(bf16[512,1024]{1,0:T(8,128)(2,1)} %q_hbm.1, bf16[512,1024]{1,0:T(8,128)(2,1)} %k_hbm.1, bf16[512,1024]{1,0:T(8,128)(2,1)} %v_hbm.1, bf16[512,1024]{1,0:T(8,128)(2,1)} %g_hbm.1, f32[8,128,128]{2,1,0:T(8,128)} %kv_hbm.1, f32[1,4096]{1,0:T(1,128)} %bitcast.3, bf16[64,1024]{1,0:T(8,128)(2,1)} %bitcast.2), custom_call_target="tpu_custom_call" | custom-call | tf_op jit(solution)/shard_map/layer/pallas_call | solution.py:415
  72.2 2.3 %copy.9 = bf16[128,4096]{1,0:T(8,128)(2,1)} copy(bf16[128,4096]{1,0:T(8,128)(2,1)} %layer.1) | data formatting | bytes 2097152

commit v3 on v2

--- a/solution.py
+++ b/solution.py
@@ -21,7 +21,7 @@
     q_hbm, k_hbm, v_hbm, g_hbm, kv_hbm, gain_hbm, w_hbm, out_ref,
     q, k, v, g, kv, gain, wt,
     s_own, s_other, t_send, t_recv, line, l_send, l_recv, p_send, p_chip, c_send, c_recv,
-    inner, gated, hidden, sq, sq_recv, terms,
+    inner, gated, hidden, squares, sq_send, sq_recv, scale, terms,
     ra_p, ra_m, rb_p, rb_m, rc_p, rc_m,
     load, wz_s, wz_r, wx_s, wx_r, wc_s, wc_r,
     sc_s, sc_r, tz_s, tz_r, lx_s, lx_r, pz_s, pz_r, cc_s, cc_r, sq_s, sq_r,
@@ -186,8 +186,9 @@
         tz(d).start()
     t_recv[z] = t_send[z]
     local(1)
+    service_b(1)
+    near_a()
     local(2)
-    service_b(1)
     local(3)
     for d in range(1, Z):
         tz(d).wait_recv()
@@ -198,8 +199,8 @@
     l_send[...] = total.astype(BF16)
     for d in (2, 1, 3):
         lx(d).start()
-    near_a()
     service_b(2)
+    far_a()
     near(0)
     local(4)
     for d in range(1, X):
@@ -212,19 +213,18 @@
     for d in (4, 3, 5, 2, 6, 1, 7):
         pz(d).start()
     p_chip[z] = p_send[z]
-    far_a()
-    far(0)
+    near(1)
+    near(2)
     service_b(3)
     local(5)
     local(6)
     local(7)
-    near(1)
+    service_a(1)
     copies[5].wait()
     copies[6].wait()
     for i in range(4):
         rows = slice(i * 128, (i + 1) * 128)
         gated[rows] = gain[...] * jax.nn.sigmoid(g[rows].astype(F32))
-    near(2)
     copies[4].wait()
     for d in range(1, Z):
         pz(d).wait_recv()
@@ -253,21 +253,25 @@
             attn = attn.astype(BF16).astype(F32)
             square = attn * attn
             if first and h == 0:
-                sq[...] = square
+                squares[...] = square
             else:
-                sq[...] += square
+                squares[...] += square
             hidden[:, cols] = (attn * gated[:, cols]).astype(BF16)
 
     finish(0, True)
+    near(3)
+    near(4)
     service_b(4)
-    service_a(1)
+    far(0)
     far(1)
     prefix_swap.wait_recv()
     finish(1, False)
-    sq[...] = jnp.broadcast_to(jnp.sum(sq[...], axis=1, keepdims=True), (512, 128))
+    for d in range(Y):
+        sums = jnp.sum(jnp.transpose(squares[y_quarter[d]]), axis=0, keepdims=True)
+        sq_send[d] = jnp.broadcast_to(sums, (8, 128))
 
     def sqs(d):
-        return remote(sq.at[y_quarter[d]], sq_recv.at[d], sq_s.at[d], sq_r.at[d], row(d))
+        return remote(sq_send.at[d], sq_recv.at[d], sq_s.at[d], sq_r.at[d], row(d))
 
     for d in range(1, Y):
         sqs(d).start()
@@ -288,83 +292,79 @@
         for side in range(2):
             weights = wt[j, pl.ds(2 * side, 2)].reshape(256, 1024)
             terms[j, side] = dot(hidden[...], weights, 1, 1).astype(BF16)
-        for kind in range(4):
-            rs(j, kind).start()
+            rs(j, side).start()
+
+    def direct(j):
+        rs(j, 2).start()
+        rs(j, 3).start()
 
     def relay(j):
-        for side, part, kind in ((0, ra_p, 0), (1, ra_m, 1)):
-            rs(j, kind).wait_recv()
-            rows = y_quarter[1 if side == 0 else 3]
+        for side, part, rows in ((0, ra_p, y_quarter[1]), (1, ra_m, y_quarter[3])):
+            rs(j, side).wait_recv()
             terms[j, side, rows] = (terms[j, side, rows].astype(F32) + part[j].astype(F32)).astype(BF16)
             rs(j, 4 + side).start()
 
-    def final(j, scale):
+    def final(j):
         for kind in (2, 3, 4, 5):
             rs(j, kind).wait_recv()
         s = (j + 1) // 2
-        zz = lax.rem(z + s * (1 - 2 * lax.rem(j, 2)) + Z, Z)
+        zz = lax.rem(z + s * (1 - 2 * (j % 2)) + Z, Z)
         for side, b, d in ((0, rb_p, rc_m), (1, rb_m, rc_p)):
             total = terms[j, side, y_quarter[0]].astype(F32) + b[j].astype(F32) + d[j].astype(F32)
             for n in range(2):
                 xx = lax.rem(x + (0, 3, 1, 2)[2 * side + n], X)
                 cols = pl.ds(pl.multiple_of((xx * Z + zz) * 128, 128), 128)
-                out_ref[:, cols] = (total[:, n * 128:(n + 1) * 128] * scale).astype(BF16)
-
-    def step(i, _):
-        @pl.when(i == 0)
-        def _():
-            near(3)
-            far(2)
-
-        @pl.when(i == 1)
-        def _():
-            near(4)
-            service_a(2)
-            far(3)
-
-        @pl.when(i == 2)
-        def _():
-            near(5)
-            far(4)
-
-        @pl.when(i == 3)
-        def _():
-            near(6)
-            service_a(3)
-            far(5)
-
-        @pl.when(i == 4)
-        def _():
-            near(7)
-            far(6)
-
-        @pl.when(i == 5)
-        def _():
-            service_a(4)
-            far(7)
-
-        @pl.when(i < 8)
-        def _():
-            project(i)
-
-        @pl.when((i >= 1) & (i < 9))
-        def _():
-            relay(i - 1)
-
-        @pl.when(i == 1)
-        def _():
-            for d in range(1, Y):
-                sqs(d).wait()
-            total = sq[y_quarter[0]] + sq_recv[1] + sq_recv[2] + sq_recv[3]
-            sq_recv[0] = lax.rsqrt(total / (Y * 1024) + EPS)
-
-        @pl.when(i >= 2)
-        def _():
-            final(i - 2, sq_recv[0])
-
-        return 0
-
-    lax.fori_loop(0, 10, step, 0)
+                out_ref[:, cols] = (total[:, n * 128:(n + 1) * 128] * scale[...]).astype(BF16)
+
+    project(0)
+    direct(0)
+    near(5)
+    near(6)
+    far(2)
+    project(1)
+    near(7)
+    service_a(2)
+    far(3)
+    relay(0)
+    project(2)
+    direct(1)
+    far(4)
+    service_a(3)
+    far(5)
+    far(6)
+    relay(1)
+    project(3)
+    direct(2)
+    service_a(4)
+    far(7)
+    for d in range(1, Y):
+        sqs(d).wait()
+    total = sq_send[0] + sq_recv[1] + sq_recv[2] + sq_recv[3]
+    factor = lax.rsqrt(total / (Y * 1024) + EPS)
+    scale[...] = jnp.transpose(jnp.broadcast_to(factor[0:1], (128, 128)))
+    relay(2)
+    project(4)
+    direct(3)
+    final(0)
+    relay(3)
+    project(5)
+    direct(4)
+    final(1)
+    relay(4)
+    project(6)
+    direct(5)
+    final(2)
+    relay(5)
+    project(7)
+    direct(6)
+    final(3)
+    relay(6)
+    direct(7)
+    final(4)
+    relay(7)
+    final(5)
+    final(6)
+    final(7)
 
     for dst in range(1, Z):
         wz(0, dst, 1).wait_send()
@@ -405,7 +405,8 @@
         pltpu.VMEM((Z, 64, DH), BF16), pltpu.VMEM((Z, 64, DH), BF16),
         pltpu.VMEM((4, DH, DH), F32), pltpu.VMEM((4, DH, DH), F32),
         pltpu.VMEM((512, 1024), F32), pltpu.VMEM((512, 1024), F32), pltpu.VMEM((512, 1024), BF16),
-        pltpu.VMEM((512, 128), F32), pltpu.VMEM((Y, 128, 128), F32),
+        pltpu.VMEM((512, 128), F32), pltpu.VMEM((Y, 8, 128), F32), pltpu.VMEM((Y, 8, 128), F32),
+        pltpu.VMEM((128, 128), F32),
         pltpu.VMEM((Z, 2, 512, 256), BF16),
     ] + [pltpu.VMEM((Z, 128, 256), BF16)] * 6 + [
         dma((7,)), dma((5, Z)), dma((5, Z)), dma((Z + 1, 4)), dma((Z + 1, 4)), dma((Z,)), dma((Z,)),

time: 75.9 us -> 74.2 us (0.978); the launches traced: 74.5 us -> 74.1 us
  no operation moved by 1% of the time
where the time goes in v3:
time: 74.2 us; the launch traced here: 74.1 us
  Pallas kernels  71.8 us (97%)
  local copies, waits for them, and re-layouts  2.29 us (3%)
    pallas_call x1, Pallas kernels, shards(): pl.pallas_call(body, out_shape=jax.ShapeDtypeStruct((128, 4096), BF16), i...  71.8 us
    unnamed x1, local copies, waits for them, and re-layouts  2.29 us

profile of v3, /device:TPU:1, one launch (start us, length us, event | category | flops | bytes accessed | tf_op | source)
XLA Modules:
  0.0 74.1 jit_solution(2909583967510975578)
XLA Ops:
  0.0 71.8 %layer.1 = bf16[128,4096]{1,0:T(8,128)(2,1)} custom-call(bf16[512,1024]{1,0:T(8,128)(2,1)} %q_hbm.1, bf16[512,1024]{1,0:T(8,128)(2,1)} %k_hbm.1, bf16[512,1024]{1,0:T(8,128)(2,1)} %v_hbm.1, bf16[512,1024]{1,0:T(8,128)(2,1)} %g_hbm.1, f32[8,128,128]{2,1,0:T(8,128)} %kv_hbm.1, f32[1,4096]{1,0:T(1,128)} %bitcast.3, bf16[64,1024]{1,0:T(8,128)(2,1)} %bitcast.2), custom_call_target="tpu_custom_call" | custom-call | tf_op jit(solution)/shard_map/layer/pallas_call | solution.py:416
  71.8 2.3 %copy.9 = bf16[128,4096]{1,0:T(8,128)(2,1)} copy(bf16[128,4096]{1,0:T(8,128)(2,1)} %layer.1) | data formatting | bytes 2097152

commit v4 on v3

--- a/solution.py
+++ b/solution.py
@@ -18,14 +18,14 @@
 
 
 def body(
-    q_hbm, k_hbm, v_hbm, g_hbm, kv_hbm, gain_hbm, w_hbm, out_ref,
-    q, k, v, g, kv, gain, wt,
+    q_hbm, k_hbm, v_hbm, g_hbm, kv_hbm, gain_hbm, w_hbm, out_hbm,
+    out_ref, q, k, v, g, kv, gain, wt,
     s_own, s_other, t_send, t_recv, line, l_send, l_recv, p_send, p_chip, c_send, c_recv,
     inner, gated, hidden, squares, sq_send, sq_recv, scale, terms,
     ra_p, ra_m, rb_p, rb_m, rc_p, rc_m,
     load, wz_s, wz_r, wx_s, wx_r, wc_s, wc_r,
     sc_s, sc_r, tz_s, tz_r, lx_s, lx_r, pz_s, pz_r, cc_s, cc_r, sq_s, sq_r,
-    rs_s, rs_r,
+    rs_s, rs_r, put_s,
 ):
     seq, y = lax.axis_index("seq"), lax.axis_index("head")
     c = lax.rem(seq, 2)
@@ -304,6 +304,13 @@
             terms[j, side, rows] = (terms[j, side, rows].astype(F32) + part[j].astype(F32)).astype(BF16)
             rs(j, 4 + side).start()
 
+    def put(j, place):
+        s = (j + 1) // 2
+        zz = lax.rem(z + s * (1 - 2 * (j % 2)) + Z, Z)
+        xx = lax.rem(x + (0, 3, 1, 2)[place], X)
+        cols = pl.ds(pl.multiple_of((xx * Z + zz) * 128, 128), 128)
+        return pltpu.make_async_copy(out_ref.at[:, cols], out_hbm.at[:, cols], put_s.at[j, place])
+
     def final(j):
         for kind in (2, 3, 4, 5):
             rs(j, kind).wait_recv()
@@ -315,6 +322,7 @@
                 xx = lax.rem(x + (0, 3, 1, 2)[2 * side + n], X)
                 cols = pl.ds(pl.multiple_of((xx * Z + zz) * 128, 128), 128)
                 out_ref[:, cols] = (total[:, n * 128:(n + 1) * 128] * scale[...]).astype(BF16)
+                put(j, 2 * side + n).start()
 
     project(0)
     direct(0)
@@ -372,6 +380,9 @@
             wz(place, dst, 0).wait_send()
     for kind in range(4):
         wx(0, kind, 0).wait_send()
+    for j in range(8):
+        for place in range(4):
+            put(j, place).wait()
     state_swap.wait_send()
     prefix_swap.wait_send()
     for d in range(1, Z):
@@ -393,9 +404,9 @@
 
 def shards(queries, key_input, value_input, gate_input, kv_state, norm_gain, out_weight):
     hbm = pl.BlockSpec(memory_space=pltpu.HBM)
-    vmem = pl.BlockSpec(memory_space=pltpu.VMEM)
     dma = pltpu.SemaphoreType.DMA
     scratch = [
+        pltpu.VMEM((128, 4096), BF16),
         pltpu.VMEM((512, 1024), BF16), pltpu.VMEM((512, 1024), BF16), pltpu.VMEM((512, 1024), BF16),
         pltpu.VMEM((512, 1024), BF16), pltpu.VMEM((8, DH, DH), F32), pltpu.VMEM((1, 1024), F32),
         pltpu.VMEM((Z, X, 2, 64, 1024), BF16),
@@ -412,12 +423,13 @@
         dma((7,)), dma((5, Z)), dma((5, Z)), dma((Z + 1, 4)), dma((Z + 1, 4)), dma((Z,)), dma((Z,)),
         dma, dma, dma((Z,)), dma((Z,)), dma((X,)), dma((X,)), dma((Z,)), dma((Z,)),
         dma, dma, dma((Y,)), dma((Y,)), dma((Z, 6)), dma((Z, 6)),
+        dma((8, 4)),
     ]
     return pl.pallas_call(
         body,
         out_shape=jax.ShapeDtypeStruct((128, 4096), BF16),
         in_specs=[hbm] * 7,
-        out_specs=vmem,
+        out_specs=hbm,
         scratch_shapes=scratch,
         compiler_params=pltpu.CompilerParams(
             collective_id=0, has_side_effects=True, vmem_limit_bytes=60 << 20

time: 74.2 us -> 74.1 us (level)
  no operation moved by 1% of the time
where the time goes in v4:
time: 74.1 us; the launch traced here: 74 us
  Pallas kernels  71.7 us (97%)
  local copies, waits for them, and re-layouts  2.29 us (3%)
    pallas_call x1, Pallas kernels, shards(): pl.pallas_call(body, out_shape=jax.ShapeDtypeStruct((128, 4096), BF16), i...  71.7 us
    unnamed x1, local copies, waits for them, and re-layouts  2.29 us

profile of v4, /device:TPU:1, one launch (start us, length us, event | category | flops | bytes accessed | tf_op | source)
XLA Modules:
  0.0 74.0 jit_solution(1042867084907112592)
XLA Ops:
  0.0 71.7 %layer.1 = bf16[128,4096]{1,0:T(8,128)(2,1)} custom-call(bf16[512,1024]{1,0:T(8,128)(2,1)} %q_hbm.1, bf16[512,1024]{1,0:T(8,128)(2,1)} %k_hbm.1, bf16[512,1024]{1,0:T(8,128)(2,1)} %v_hbm.1, bf16[512,1024]{1,0:T(8,128)(2,1)} %g_hbm.1, f32[8,128,128]{2,1,0:T(8,128)} %kv_hbm.1, f32[1,4096]{1,0:T(1,128)} %bitcast.3, bf16[64,1024]{1,0:T(8,128)(2,1)} %bitcast.2), custom_call_target="tpu_custom_call" | custom-call | tf_op jit(solution)/shard_map/layer/pallas_call | solution.py:428
  71.7 2.3 %copy.9 = bf16[128,4096]{1,0:T(8,128)(2,1)} copy(bf16[128,4096]{1,0:T(8,128)(2,1)} %layer.1) | data formatting | bytes 2097152
